TPU v7x, 32 devices: a whole 2x2x4 slice. The times are simulated.
32 devices in a mesh: groups: 2 (over y), path: 4 (over z), half: 2 (over x), tile: 2 (over core).
Axes of the slice: x: 2, y: 2, z: 4, core: 2. Of those that a mesh axis runs over, the one named last changes fastest.
Arguments:
- left_prefix: bfloat16 [64, 4096], P(('groups', 'path'), ('half', 'tile')), parts along dimension 0, may hold values from -6 to 6
- right_prefix: bfloat16 [64, 4096], P(('groups', 'half', 'tile'), 'path'), parts along dimension 0, may hold values from -6 to 6
- left_layer: bfloat16 [2048, 1024], P(('groups', 'half', 'tile')), parts along dimension 0, may hold values from -0.1875 to 0.1875
- right_layer: bfloat16 [2048, 1024], P(('groups', 'path')), parts along dimension 0, may hold values from -0.1875 to 0.1875
- left_map: int32 [512], P('groups'), parts along dimension 0, may hold values from 0 to 31
- right_map: int32 [512], P('groups'), parts along dimension 0, may hold values from 0 to 31
- branch_bits: int32 [512, 10], P('groups'), parts along dimension 0, may hold values 0 or 1
- cut_side: int32 [20], P('groups'), parts along dimension 0, may hold values 0 or 1
Outputs:
- amplitude: bfloat16 [8192, 4096], P(('groups', 'half', 'tile'), 'path'), parts along dimension 0
There are 2 independent parts, one for each index of `groups`. A program takes and returns all parts, laid end to end along the dimension named above; each array names one. Nothing has to cross between parts.
All inputs are finite; a program needn't handle non-finite values.
Results may differ from a plain program's by a relative error of at most 0.0058.
Values may be sent and summed in bfloat16 or wider, within the bound.
A program may use at most 64 MiB of HBM per device.

v0:
```python
import jax
import jax.numpy as jnp
from jax import lax
from jax.sharding import PartitionSpec as P


def cut_factors(branch, cut_side, gate_count, on_left):
    cut_count = cut_side.shape[0]
    bit_place = lax.broadcasted_iota(jnp.int32, (cut_count, gate_count), 0)
    gate_code = lax.broadcasted_iota(jnp.int32, (cut_count, gate_count), 1)
    bit_table = jnp.right_shift(gate_code, bit_place) & 1
    projector = cut_side if on_left else 1 - cut_side
    phased = 1 - projector
    chosen = branch * projector[None, :]
    misses = (
        jnp.sum(chosen, axis=1, keepdims=True)
        + jnp.dot(projector, bit_table)[None, :]
        - 2 * jnp.dot(chosen, bit_table)
    )
    parity = jnp.dot(branch * phased[None, :], bit_table)
    sign_value = 1 - 2 * (parity % 2)
    return jnp.where(misses == 0, sign_value, 0).astype(jnp.bfloat16)


def project(prefix_rows, path_map, branch, cut_side, on_left):
    factor = cut_factors(branch, cut_side, prefix_rows.shape[1], on_left)
    return prefix_rows[path_map] * factor


def apply_left(projected, left_layer):

    def columns(layer_piece, first_row):
        return lax.dot_general(
            projected, layer_piece, (((1,), (1,)), ((), ())), preferred_element_type=jnp.float32
        )

    states = columns(lax.all_gather(left_layer, ("half", "tile"), axis=0, tiled=True), jnp.int32(0))
    return states.astype(jnp.bfloat16)


def apply_right(projected, right_layer):

    def columns(layer_piece, first_row):
        return lax.dot_general(
            projected, layer_piece, (((1,), (1,)), ((), ())), preferred_element_type=jnp.float32
        )

    states = columns(lax.all_gather(right_layer, "path", axis=0, tiled=True), jnp.int32(0))
    return states.astype(jnp.bfloat16)


def on_device(
    left_prefix, right_prefix, left_layer, right_layer, left_map, right_map, branch_bits, cut_side
):
    left_rows = lax.all_gather(left_prefix, "path", axis=0, tiled=True)
    right_rows = lax.all_gather(right_prefix, ("half", "tile"), axis=0, tiled=True)
    left_states = apply_left(project(left_rows, left_map, branch_bits, cut_side, True), left_layer)
    right_states = apply_right(
        project(right_rows, right_map, branch_bits, cut_side, False), right_layer
    )
    amplitude = lax.dot_general(
        left_states, right_states, (((0,), (0,)), ((), ())), preferred_element_type=jnp.float32
    )
    return amplitude.astype(jnp.bfloat16)


def solution(mesh):
    in_specs = (
        P(("groups", "path"), ("half", "tile")),
        P(("groups", "half", "tile"), "path"),
        P(("groups", "half", "tile"), None),
        P(("groups", "path"), None),
        P("groups"),
        P("groups"),
        P("groups", None),
        P("groups"),
    )
    out_specs = P(("groups", "half", "tile"), "path")
    return jax.shard_map(
        on_device, mesh=mesh, in_specs=in_specs, out_specs=out_specs, check_vma=False
    )
```

profile of v0, /device:TPU:0, one launch (start us, length us, event | category | flops | bytes accessed | tf_op | source)
XLA Modules:
  0.0 92.8 jit_solution(1956754094180607474)
XLA Ops:
  6.5 0.0 all-gather.5.cloned.1.call-start
  6.5 0.7 all-gather.5.cloned.1.call-update
  7.3 0.0 all-gather.3.cloned.1.call-start
  7.3 0.7 all-gather.3.cloned.1.call-update
  8.0 6.5 %all_gather.14 = bf16[32,1024]{1,0:T(8,128)(2,1)S(1)} all-gather(bf16[8,1024]{1,0:T(8,128)(2,1)} %param.9), channel_id=1, replica_groups=mesh['groups'=2,'path'=4,'half'=2,'tile'=2] {'half','tile'}, dimensions={0}, use_global_device_ids=true | all-gather | bytes 81920 | tf_op jit(solution)/shard_map/all_gather | solution.py:56
  14.5 0.7 compare_select_fusion
  15.2 0.0 copy-start.1
  15.2 0.0 copy-start.3
  15.2 1.2 %gather_fusion.1 = bf16[256,1024]{1,0:T(8,128)(2,1)S(1)} fusion(bf16[32,1024]{1,0:T(8,128)(2,1)S(1)} %all_gather.14, s32[1024]{0:T(1024)S(1)} %pad_clamp_fusion), kind=kCustom, calls=%fused_computation.1 | custom fusion | bytes 1049600 | tf_op jit(solution)/shard_map/gather | solution.py:27
  16.3 0.0 copy-done.1
  16.3 14.5 %all_gather.12 = bf16[32,1024]{1,0:T(8,128)(2,1)S(1)} all-gather(bf16[8,1024]{1,0:T(8,128)(2,1)S(1)} %copy-done.1), channel_id=1, replica_groups=mesh['groups'=2,'path'=4,'half'=2,'tile'=2] {'path'}, dimensions={0}, use_global_device_ids=true | all-gather | bytes 81920 | tf_op jit(solution)/shard_map/all_gather | solution.py:55
  30.8 0.0 copy-done.3
  30.8 0.0 copy-start.2
  30.9 0.0 copy-start
  30.9 1.2 %gather_fusion = bf16[256,1024]{1,0:T(8,128)(2,1)S(1)} fusion(bf16[32,1024]{1,0:T(8,128)(2,1)S(1)} %all_gather.12, s32[1024]{0:T(1024)S(1)} %pad_clamp_fusion.1), kind=kCustom, calls=%fused_computation | custom fusion | bytes 1049600 | tf_op jit(solution)/shard_map/gather | solution.py:27
  32.0 0.0 copy-done.2
  32.1 0.0 copy-done
  32.1 0.1 multiply_reduce_fusion.1
  32.2 0.2 fusion.28
  32.3 0.2 fusion.31
  32.5 1.7 %fusion.29 = s32[256,1024]{1,0:T(8,128)S(1)} fusion(s32[256,10]{0,1:T(8,128)S(1)} %copy-done, s32[10]{0:T(128)S(1)} %broadcast_subtract_fusion), kind=kOutput, calls=%fused_computation.35 | convolution fusion | flops 5265920 | bytes 1058856 | tf_op jit(solution)/shard_map/dot_general | solution.py:20
  34.2 1.7 %fusion.30 = s32[256,1024]{1,0:T(8,128)S(1)} fusion(s32[256,10]{0,1:T(8,128)S(1)} %copy-done, s32[10]{0:T(128)S(1)} %copy-done.2), kind=kOutput, calls=%fused_computation.36 | convolution fusion | flops 5265920 | bytes 1058856 | tf_op jit(solution)/shard_map/dot_general | solution.py:18
  35.9 22.1 %all-gather.5.cloned.1.call-done = bf16[1024,1024]{1,0:T(8,128)(2,1)} async-done(((bf16[256,1024]{1,0:T(8,128)(2,1)}), bf16[1024,1024]{1,0:T(8,128)(2,1)}) %all-gather.5.cloned.1.call-update) | async-done | bytes 2097168 | tf_op jit(solution)/shard_map/all_gather | solution.py:48
  58.0 3.6 %convolution_convert_fusion.1 = bf16[256,1024]{1,0:T(8,128)(2,1)} fusion(bf16[1024,1024]{1,0:T(8,128)(2,1)} %all-gather.5.cloned.1.call-done, bf16[256,1024]{1,0:T(8,128)(2,1)S(1)} %gather_fusion.1, s32[256,1024]{1,0:T(8,128)S(1)} %fusion.29, s32[256,1024]{1,0:T(8,128)S(1)} %fusion.30, s32[1024]{0:T(1024)S(1)} %bitcast.12, s32[256]{0:T(256)S(1)} %get-tuple-element.6), kind=kOutput, calls=%fused_computation.9 | convolution fusion | flops 543162368 | bytes 5248000 | tf_op jit(solution)/shard_map/dot_general | solution.py:44
  61.7 19.5 %all-gather.3.cloned.1.call-done = bf16[1024,1024]{1,0:T(8,128)(2,1)} async-done(((bf16[256,1024]{1,0:T(8,128)(2,1)}), bf16[1024,1024]{1,0:T(8,128)(2,1)}) %all-gather.3.cloned.1.call-update) | async-done | bytes 2097168 | tf_op jit(solution)/shard_map/all_gather | solution.py:37
  81.2 4.8 %convolution_convert_fusion = bf16[1024,1024]{1,0:T(8,128)(2,1)} fusion(bf16[256,1024]{1,0:T(8,128)(2,1)} %convolution_convert_fusion.1, bf16[1024,1024]{1,0:T(8,128)(2,1)} %all-gather.3.cloned.1.call-done, bf16[256,1024]{1,0:T(8,128)(2,1)S(1)} %gather_fusion, s32[256,1024]{1,0:T(8,128)S(1)} %fusion.30, s32[256,1024]{1,0:T(8,128)S(1)} %fusion.29, ...), kind=kOutput, calls=%fused_computation.2 | convolution fusion | flops 1081081856 | bytes 7345152 | tf_op jit(solution)/shard_map/dot_general | solution.py:61
  (4 shorter events, 0.0 us)
Async XLA Ops:
  6.5 51.5 %all-gather.5.cloned.1.call-start = ((), (), s32[]{:S(2)}) async-start(), calls=%async_computation.1 | async-start | bytes 2621440 | tf_op jit(solution)/shard_map/all_gather | solution.py:48
  7.3 73.9 %all-gather.3.cloned.1.call-start = ((), (), s32[]{:S(2)}) async-start(), calls=%async_computation | async-start | bytes 2621440 | tf_op jit(solution)/shard_map/all_gather | solution.py:37
  15.2 1.2 %copy-start.1 = (bf16[8,1024]{1,0:T(8,128)(2,1)S(1)}, bf16[8,1024]{1,0:T(8,128)(2,1)}, u32[]{:S(2)}) copy-start(bf16[8,1024]{1,0:T(8,128)(2,1)} %param.8) | copy-start | bytes 49156
  15.2 15.7 %copy-start.3 = (s32[256]{0:T(256)S(1)}, s32[256]{0:T(256)}, u32[]{:S(2)}) copy-start(s32[256]{0:T(256)} %param.12) | copy-start | bytes 3076
  30.8 1.2 %copy-start.2 = (s32[10]{0:T(128)S(1)}, s32[10]{0:T(128)}, u32[]{:S(2)}) copy-start(s32[10]{0:T(128)} %param.15) | copy-start | bytes 124
  30.9 1.2 %copy-start = (s32[256,10]{0,1:T(8,128)S(1)}, s32[256,10]{0,1:T(8,128)}, u32[]{:S(2)}) copy-start(s32[256,10]{0,1:T(8,128)} %param.14) | copy-start | bytes 30724
Sparse Core Ops, SparseCore 0:
  8.9 49.0 all-gather.4
  59.6 21.5 all-gather.2
where the time goes:
time: 93 us; the launch traced here: 92.8 us
  waiting for transfers between devices  43 us (46%)
  blocking collectives  20.9 us (22%)
  between operations  13.5 us (15%)
  matrix products  12.2 us (13%)
  local copies, waits for them, and re-layouts  2.36 us (3%)
    all_gather x1, waiting for transfers between devices, apply_right(): lax.all_gather(right_layer, 'path', axis=0, tiled=True)  22.1 us
    all_gather x1, waiting for transfers between devices, apply_left(): lax.all_gather(left_layer, ('half', 'tile'), axis=0, tiled=True)  19.5 us
    all_gather x1, blocking collectives, on_device(): left_rows = lax.all_gather(left_prefix, 'path', axis=0, tiled=True)  14.5 us
    all_gather x1, blocking collectives, on_device(): lax.all_gather(right_prefix, ('half', 'tile'), axis=0, tiled=True)  6.46 us
    dot_general x1, matrix products, on_device(): lax.dot_general(left_states, right_states, (((0,), (0,)), ((), ())), pref...  4.84 us
    dot_general x1, matrix products, columns(): lax.dot_general(projected, layer_piece, (((1,), (1,)), ((), ())), preferr...  3.64 us
    gather x2, local copies, waits for them, and re-layouts, project(): return prefix_rows[path_map] * factor  2.34 us
  transfers between devices with their start and end apart: 2, of which 2 were waited for; matrix products, arithmetic and copies ran while one was open for 11% of the time, Pallas kernels for 0%

commit v1 on v0

--- a/solution.py
+++ b/solution.py
@@ -2,6 +2,37 @@
 import jax.numpy as jnp
 from jax import lax
 from jax.sharding import PartitionSpec as P
+
+
+def list_the_works(z, net_axis, d_out):
+    block_next = lax.axis_size(net_axis)
+    response, kept_arr, earlier = (block_next, lax.axis_index(net_axis), z.shape[d_out])
+    answer = lax.dynamic_update_slice_in_dim(
+        jnp.zeros(
+            [rr * response if tick == d_out else rr for tick, rr in enumerate(z.shape)], z.dtype
+        ),
+        z,
+        kept_arr * earlier,
+        axis=d_out,
+    )
+    z_new = now = z
+    for s in range(1, response // 2 + 1):
+        z_new = lax.ppermute(
+            z_new, net_axis, list(map(lambda tick: (tick, (tick + 1) % response), range(response)))
+        )
+        answer = lax.dynamic_update_slice_in_dim(
+            answer, z_new, (kept_arr - s) % response * earlier, axis=d_out
+        )
+        if 2 * s < response:
+            now = lax.ppermute(
+                now,
+                net_axis,
+                list(map(lambda tick: (tick, (tick - 1) % response), range(response))),
+            )
+            answer = lax.dynamic_update_slice_in_dim(
+                answer, now, (kept_arr + s) % response * earlier, axis=d_out
+            )
+    return answer
 
 
 def cut_factors(branch, cut_side, gate_count, on_left):
@@ -45,7 +76,7 @@
             projected, layer_piece, (((1,), (1,)), ((), ())), preferred_element_type=jnp.float32
         )
 
-    states = columns(lax.all_gather(right_layer, "path", axis=0, tiled=True), jnp.int32(0))
+    states = columns(list_the_works(right_layer, "path", 0), jnp.int32(0))
     return states.astype(jnp.bfloat16)
 
 

time: 93 us -> 76.5 us (0.82)
  waiting for transfers between devices: 43 us -> 0.72 us
  blocking collectives: 20.9 us -> 34.2 us
  local copies, waits for them, and re-layouts: 2.36 us -> 7.86 us
  starting transfers between devices: 0.04 us -> 5.26 us
  other arithmetic: 0.79 us -> 2.12 us
    all_gather x1 -> x0, waiting for transfers between devices: 22.1 us -> none  [apply_right(): lax.all_gather(right_layer, 'path', axis=0, tiled=True)]
    all_gather x1, waiting for transfers between devices: 19.5 us -> 0.01 us  [apply_left(): lax.all_gather(left_layer, ('half', 'tile'), axis=0, tiled=True)]
    all_gather x1, blocking collectives: 14.5 us -> 28.8 us  [on_device(): left_rows = lax.all_gather(left_prefix, 'path', axis=0, tiled=True)]
    ppermute x0 -> x3, starting transfers between devices: none -> 5.26 us  [the longest x2 3.16 us: list_the_works(): lax.ppermute(z_new, net_axis, list(map(lambda tick: (tick, (tick + 1) % r...]
    dynamic_update_slice x0 -> x4, local copies, waits for them, and re-layouts: none -> 3.67 us  [the longest x2 2.54 us: list_the_works(): lax.dynamic_update_slice_in_dim(answer, z_new, (kept_arr - s) % response...]
    gather x2, local copies, waits for them, and re-layouts: 2.34 us -> 3.91 us  [project(): return prefix_rows[path_map] * factor]
    dot_general x1, matrix products: 3.64 us -> 2.07 us  [columns(): lax.dot_general(projected, layer_piece, (((1,), (1,)), ((), ())), preferr...]
    dot_general x2, matrix products: 0.37 us -> 1.69 us  [cut_factors(): jnp.dot(projector, bit_table)[None, :]]
  transfers between devices with their start and end apart: 2 -> 4, of which waited for: 2 -> 0; matrix products, arithmetic and copies ran while one was open for 11% -> 22% of each run, Pallas kernels for 0% -> 0%
where the time goes in v1:
time: 76.5 us; the launch traced here: 76.2 us
  blocking collectives  34.2 us (45%)
  between operations  13.6 us (18%)
  matrix products  12.4 us (16%)
  local copies, waits for them, and re-layouts  7.86 us (10%)
  starting transfers between devices  5.26 us (7%)
  other arithmetic  2.12 us (3%)
    all_gather x1, blocking collectives, on_device(): left_rows = lax.all_gather(left_prefix, 'path', axis=0, tiled=True)  28.8 us
    all_gather x1, blocking collectives, on_device(): lax.all_gather(right_prefix, ('half', 'tile'), axis=0, tiled=True)  5.45 us
    dot_general x1, matrix products, on_device(): lax.dot_general(left_states, right_states, (((0,), (0,)), ((), ())), pref...  5.32 us
    gather x2, local copies, waits for them, and re-layouts, project(): return prefix_rows[path_map] * factor  3.91 us
    ppermute x2, starting transfers between devices, list_the_works(): lax.ppermute(z_new, net_axis, list(map(lambda tick: (tick, (tick + 1) % r...  3.16 us
    dynamic_update_slice x2, local copies, waits for them, and re-layouts, list_the_works(): lax.dynamic_update_slice_in_dim(answer, z_new, (kept_arr - s) % response...  2.54 us
    ppermute x1, starting transfers between devices, list_the_works(): lax.ppermute(now, net_axis, list(map(lambda tick: (tick, (tick - 1) % res...  2.09 us
    dot_general x1, matrix products, columns(): lax.dot_general(projected, layer_piece, (((1,), (1,)), ((), ())), preferr...  2.07 us
  transfers between devices with their start and end apart: 4, of which 0 were waited for; matrix products, arithmetic and copies ran while one was open for 22% of the time, Pallas kernels for 0%

profile of v1, /device:TPU:0, one launch (start us, length us, event | category | flops | bytes accessed | tf_op | source)
XLA Modules:
  0.0 76.2 jit_solution(9448678437118422326)
XLA Ops:
  6.5 0.0 all-gather.2.cloned.1.call-start
  6.5 0.7 all-gather.2.cloned.1.call-update
  7.3 3.1 %collective-permute-start = (bf16[256,1024]{1,0:T(8,128)(2,1)}, bf16[256,1024]{1,0:T(8,128)(2,1)}, u32[]{:S(2)}, u32[]{:S(2)}) collective-permute-start(bf16[256,1024]{1,0:T(8,128)(2,1)} %param.11), channel_id=1, source_target_pairs={{0,4},{4,8},{8,12},{12,0},{1,5},{5,9},{9,13},{13,1},{2,6},{6,10},{... | collective-permute-start | bytes 1572872 | tf_op jit(solution)/shard_map/ppermute | solution.py:20
  10.4 2.1 %collective-permute-start.1 = (bf16[256,1024]{1,0:T(8,128)(2,1)}, bf16[256,1024]{1,0:T(8,128)(2,1)}, u32[]{:S(2)}, u32[]{:S(2)}) collective-permute-start(bf16[256,1024]{1,0:T(8,128)(2,1)} %param.11), channel_id=1, source_target_pairs={{0,12},{4,0},{8,4},{12,8},{1,13},{5,1},{9,5},{13,9},{2,14},{6,2},{... | collective-permute-start | bytes 1572872 | tf_op jit(solution)/shard_map/ppermute | solution.py:27
  12.5 0.7 compare_select_fusion
  13.1 0.7 broadcast_subtract_fusion
  13.8 0.7 compare_select_fusion.1
  14.5 0.8 %fusion.28 = s32[1,1024]{1,0:T(1,128)S(1)} fusion(s32[10]{0:T(128)} %param.15), kind=kOutput, calls=%fused_computation.34 | convolution fusion | flops 40970 | bytes 4136 | tf_op jit(solution)/shard_map/dot_general | solution.py:48
  15.3 0.8 %fusion.31 = s32[1,1024]{1,0:T(1,128)S(1)} fusion(s32[10]{0:T(128)} %param.15), kind=kOutput, calls=%fused_computation.37 | convolution fusion | flops 40960 | bytes 4136 | tf_op jit(solution)/shard_map/dot_general | solution.py:48
  16.3 5.4 %all_gather.11 = bf16[32,1024]{1,0:T(8,128)(2,1)S(1)} all-gather(bf16[8,1024]{1,0:T(8,128)(2,1)} %param.9), channel_id=1, replica_groups=mesh['groups'=2,'path'=4,'half'=2,'tile'=2] {'half','tile'}, dimensions={0}, use_global_device_ids=true | all-gather | bytes 81920 | tf_op jit(solution)/shard_map/all_gather | solution.py:87
  21.7 0.0 copy-start.3
  21.7 0.0 copy-start.5
  21.7 2.0 %gather_fusion.1 = bf16[256,1024]{1,0:T(8,128)(2,1)} fusion(bf16[32,1024]{1,0:T(8,128)(2,1)S(1)} %all_gather.11, s32[1024]{0:T(1024)S(1)} %pad_clamp_fusion), kind=kCustom, calls=%fused_computation.1 | custom fusion | bytes 1049600 | tf_op jit(solution)/shard_map/gather | solution.py:58
  23.7 0.0 copy-done.3
  23.7 0.0 copy-done.5
  23.7 0.0 copy-start.2
  23.7 0.1 multiply_reduce_fusion.1
  23.8 0.0 copy-start.4
  23.8 1.7 %fusion.29 = s32[256,1024]{1,0:T(8,128)S(1)} fusion(s32[256,10]{0,1:T(8,128)S(1)} %copy-done.3, s32[10]{0:T(128)S(1)} %broadcast_subtract_fusion), kind=kOutput, calls=%fused_computation.35 | convolution fusion | flops 5265920 | bytes 1058856 | tf_op jit(solution)/shard_map/dot_general | solution.py:51
  25.4 0.3 broadcast_in_dim.11
  25.7 0.0 copy-done.2
  25.8 0.0 collective-permute-done
  25.8 0.1 collective-permute-start.2
  25.9 0.0 copy-done.4
  25.9 28.8 %all_gather.9 = bf16[32,1024]{1,0:T(8,128)(2,1)S(1)} all-gather(bf16[8,1024]{1,0:T(8,128)(2,1)S(1)} %copy-done.4), channel_id=1, replica_groups=mesh['groups'=2,'path'=4,'half'=2,'tile'=2] {'path'}, dimensions={0}, use_global_device_ids=true | all-gather | bytes 81920 | tf_op jit(solution)/shard_map/all_gather | solution.py:86
  54.6 2.0 %gather_fusion = bf16[256,1024]{1,0:T(8,128)(2,1)} fusion(bf16[32,1024]{1,0:T(8,128)(2,1)S(1)} %all_gather.9, s32[1024]{0:T(1024)S(1)} %pad_clamp_fusion.1), kind=kCustom, calls=%fused_computation | custom fusion | bytes 1049600 | tf_op jit(solution)/shard_map/gather | solution.py:58
  56.6 0.0 copy-start.1
  56.6 1.7 %fusion.30 = s32[256,1024]{1,0:T(8,128)S(1)} fusion(s32[256,10]{0,1:T(8,128)S(1)} %copy-done.3, s32[10]{0:T(128)S(1)} %copy-done.5), kind=kOutput, calls=%fused_computation.36 | convolution fusion | flops 5265920 | bytes 1058856 | tf_op jit(solution)/shard_map/dot_general | solution.py:49
  58.3 0.0 copy-start
  58.3 1.5 %constant_dynamic-update-slice_fusion.2 = bf16[1024,1024]{1,0:T(8,128)(2,1)S(1)} fusion(bf16[1024,1024]{1,0:T(8,128)(2,1)S(1)} %constant_dynamic-update-slice_fusion.3, bf16[256,1024]{1,0:T(8,128)(2,1)} %collective-permute-done, s32[]{:T(128)S(6)} %select_n.58), kind=kLoop, calls=%fused_computation.55 | loop fusion | bytes 1048580 | tf_op jit(solution)/shard_map/dynamic_update_slice | solution.py:23
  59.7 0.0 collective-permute-done.1
  59.8 1.1 %constant_dynamic-update-slice_fusion.1 = bf16[1024,1024]{1,0:T(8,128)(2,1)S(1)} fusion(bf16[1024,1024]{1,0:T(8,128)(2,1)S(1)} %constant_dynamic-update-slice_fusion.2, bf16[256,1024]{1,0:T(8,128)(2,1)} %collective-permute-done.1, s32[]{:T(128)S(6)} %select_n.60), kind=kLoop, calls=%fused_computation.54 | loop fusion | bytes 1048580 | tf_op jit(solution)/shard_map/dynamic_update_slice | solution.py:32
  60.8 0.0 collective-permute-done.2
  60.9 1.1 %constant_dynamic-update-slice_fusion = bf16[1024,1024]{1,0:T(8,128)(2,1)S(1)} fusion(bf16[1024,1024]{1,0:T(8,128)(2,1)S(1)} %constant_dynamic-update-slice_fusion.1, bf16[256,1024]{1,0:T(8,128)(2,1)} %collective-permute-done.2, s32[]{:T(128)S(6)} %select_n.62), kind=kLoop, calls=%fused_computation.53 | loop fusion | bytes 1048580 | tf_op jit(solution)/shard_map/dynamic_update_slice | solution.py:23
  61.9 0.0 copy-done
  61.9 0.0 copy-done.1
  62.0 2.1 %convolution_convert_fusion.1 = bf16[256,1024]{1,0:T(8,128)(2,1)} fusion(bf16[1024,1024]{1,0:T(8,128)(2,1)S(1)} %constant_dynamic-update-slice_fusion, bf16[256,1024]{1,0:T(8,128)(2,1)S(1)} %copy-done.1, s32[256,1024]{1,0:T(8,128)S(1)} %fusion.29, s32[256,1024]{1,0:T(8,128)S(1)} %fusion.30, s32[1024]{0:T(1024)S(1)} %bitcast.12, s32[256]{0:T(256)S(1)} %get-tuple-element.6), kind=kOutput, calls=%fused_computation.9 | convolution fusion | flops 543162368 | bytes 5248000 | tf_op jit(solution)/shard_map/dot_general | solution.py:75
  64.0 0.0 all-gather.2.cloned.1.call-done
  64.0 5.3 %convolution_convert_fusion = bf16[1024,1024]{1,0:T(8,128)(2,1)} fusion(bf16[256,1024]{1,0:T(8,128)(2,1)} %convolution_convert_fusion.1, bf16[1024,1024]{1,0:T(8,128)(2,1)} %all-gather.2.cloned.1.call-done, bf16[256,1024]{1,0:T(8,128)(2,1)} %gather_fusion, s32[256,1024]{1,0:T(8,128)} %copy-done, s32[256,1024]{1,0:T(8,128)S(1)} %fusion.29, ...), kind=kOutput, calls=%fused_computation.2 | convolution fusion | flops 1081081856 | bytes 7345152 | tf_op jit(solution)/shard_map/dot_general | solution.py:92
  (3 shorter events, 0.1 us)
Async XLA Ops:
  6.5 57.5 %all-gather.2.cloned.1.call-start = ((), (), s32[]{:S(2)}) async-start(), calls=%async_computation | async-start | bytes 2621440 | tf_op jit(solution)/shard_map/all_gather | solution.py:68
  7.3 18.5 %collective-permute-start = (bf16[256,1024]{1,0:T(8,128)(2,1)}, bf16[256,1024]{1,0:T(8,128)(2,1)}, u32[]{:S(2)}, u32[]{:S(2)}) collective-permute-start(bf16[256,1024]{1,0:T(8,128)(2,1)} %param.11), channel_id=1, source_target_pairs={{0,4},{4,8},{8,12},{12,0},{1,5},{5,9},{9,13},{13,1},{2,6},{6,10},{... | collective-permute-start | bytes 1572872 | tf_op jit(solution)/shard_map/ppermute | solution.py:20
  10.4 49.4 %collective-permute-start.1 = (bf16[256,1024]{1,0:T(8,128)(2,1)}, bf16[256,1024]{1,0:T(8,128)(2,1)}, u32[]{:S(2)}, u32[]{:S(2)}) collective-permute-start(bf16[256,1024]{1,0:T(8,128)(2,1)} %param.11), channel_id=1, source_target_pairs={{0,12},{4,0},{8,4},{12,8},{1,13},{5,1},{9,5},{13,9},{2,14},{6,2},{... | collective-permute-start | bytes 1572872 | tf_op jit(solution)/shard_map/ppermute | solution.py:27
  21.7 2.0 %copy-start.3 = (s32[256,10]{0,1:T(8,128)S(1)}, s32[256,10]{0,1:T(8,128)}, u32[]{:S(2)}) copy-start(s32[256,10]{0,1:T(8,128)} %param.14) | copy-start | bytes 30724
  21.7 2.0 %copy-start.5 = (s32[10]{0:T(128)S(1)}, s32[10]{0:T(128)}, u32[]{:S(2)}) copy-start(s32[10]{0:T(128)} %param.15) | copy-start | bytes 124
  23.7 2.0 %copy-start.2 = (bf16[256,1024]{1,0:T(8,128)(2,1)S(1)}, bf16[256,1024]{1,0:T(8,128)(2,1)}, u32[]{:S(2)}) copy-start(bf16[256,1024]{1,0:T(8,128)(2,1)} %param.11) | copy-start | bytes 1572868
  23.8 2.1 %copy-start.4 = (bf16[8,1024]{1,0:T(8,128)(2,1)S(1)}, bf16[8,1024]{1,0:T(8,128)(2,1)}, u32[]{:S(2)}) copy-start(bf16[8,1024]{1,0:T(8,128)(2,1)} %param.8) | copy-start | bytes 49156
  25.8 35.1 %collective-permute-start.2 = (bf16[256,1024]{1,0:T(8,128)(2,1)}, bf16[256,1024]{1,0:T(8,128)(2,1)}, u32[]{:S(2)}, u32[]{:S(2)}) collective-permute-start(bf16[256,1024]{1,0:T(8,128)(2,1)} %collective-permute-done), channel_id=1, source_target_pairs={{0,4},{4,8},{8,12},{12,0},{1,5},{5,9},{9,13},{13,1},{2,6},{6,10},{... | collective-permute-start | bytes 1572872 | tf_op jit(solution)/shard_map/ppermute | solution.py:20
  56.6 5.4 %copy-start.1 = (bf16[256,1024]{1,0:T(8,128)(2,1)S(1)}, bf16[256,1024]{1,0:T(8,128)(2,1)}, u32[]{:S(2)}) copy-start(bf16[256,1024]{1,0:T(8,128)(2,1)} %gather_fusion.1) | copy-start | bytes 1572868
  58.3 3.7 %copy-start = (s32[256,1024]{1,0:T(8,128)}, s32[256,1024]{1,0:T(8,128)S(1)}, u32[]{:S(2)}) copy-start(s32[256,1024]{1,0:T(8,128)S(1)} %fusion.30) | copy-start | bytes 3145732
Sparse Core Ops, SparseCore 0:
  8.9 25.2 all-gather.1
